TPU v7x, 32 devices: a whole 2x2x4 slice. The times are simulated.
32 devices in a mesh: section: 2 (over core), expert: 8 (over z, x), dp: 2 (over y).
Axes of the slice: x: 2, y: 2, z: 4, core: 2. Of those that a mesh axis runs over, the one named last changes fastest.
Arguments:
- tokens: bfloat16 [4, 512, 2048], P(None, ('expert', 'dp')), may hold values from -6 to 6
- routes: int32 [2, 4, 512, 2], P('section', None, ('expert', 'dp')), may hold values from 0 to 7, all different within a row; in each aligned block of 32 rows (0 to 31, 32 to 63, ..., all dimensions but the last counted through in order) at most 9 rows name the same one
- gate_probs: float32 [2, 4, 512, 2], P('section', None, ('expert', 'dp')), may hold values from 0.1 to 1
- w_gate: bfloat16 [2, 8, 2048, 640], P('section', 'expert'), may hold values from -0.125 to 0.125
- w_up: bfloat16 [2, 8, 2048, 640], P('section', 'expert'), may hold values from -0.125 to 0.125
- w_down: bfloat16 [2, 8, 640, 2048], P('section', 'expert'), may hold values from -0.25 to 0.25
- cotangent: bfloat16 [4, 512, 2048], P(None, ('expert', 'dp')), may hold values from -0.29882812 to 0.29882812
Outputs:
- grad_gate: float32 [2, 8, 2048, 640], P('section', 'expert', 'dp')
- grad_up: float32 [2, 8, 2048, 640], P('section', 'expert', 'dp')
- grad_down: float32 [2, 8, 640, 2048], P('section', 'expert', None, 'dp')
Inputs may be any that keep to these rules, and one draw needn't show every extreme that they name: `routes`: in each micro-batch and layer, the 32 token rows of one device (aligned blocks) name each expert at most 9 times, a bound that some block reaches; the 2 experts of a token differ.
All inputs are finite; a program needn't handle non-finite values.
Results may differ from a plain program's by a relative error of at most 0.015.
Values may be sent and summed in bfloat16 or wider, within the bound.
No kernel may reach another device: no remote copies, remote signals or barrier semaphores. Data moves between devices by JAX's collectives and lax.ppermute only.
A program may use at most 64 MiB of HBM per device.

v0:
```python
import jax
import jax.numpy as jnp
from jax import lax
from jax.sharding import PartitionSpec as P

epsilon = 1e-05
contract_rows = (((0,), (0,)), ((), ()))
contract_cols = (((1,), (1,)), ((), ()))


def shifted(value, axis, by):
    size = lax.axis_size(axis)
    pairs = [(i, i + by) for i in range(size) if 0 <= i + by < size]
    return lax.ppermute(value, axis, pairs)


def inverse_rms(values):
    return lax.rsqrt(jnp.mean(values * values, -1, keepdims=True) + epsilon)


def slot_selector(route_ids, experts, cap_slots):
    row_count, top_k = route_ids.shape
    flat_ids = route_ids.reshape(-1)
    one_hot = (flat_ids[:, None] == jnp.arange(experts, dtype=jnp.int32)[None, :]).astype(jnp.int32)
    earlier = jnp.cumsum(one_hot, 0) - one_hot
    slot_num = jnp.sum(earlier * one_hot, 1)
    target = (flat_ids * cap_slots + slot_num).reshape(row_count, top_k)
    columns = jnp.arange(experts * cap_slots, dtype=jnp.int32)
    return (target[:, :, None] == columns[None, None, :]).astype(jnp.bfloat16)


def keep_entry(store, value, position, is_live):
    previous = lax.dynamic_index_in_dim(store, position, 0, keepdims=False)
    return lax.dynamic_update_index_in_dim(store, jnp.where(is_live, value, previous), position, 0)


def shards(tokens, routes, gate_probs, w_gate, w_up, w_down, cotangent):
    micro_count, row_count, model_width = tokens.shape
    top_k = routes.shape[-1]
    experts = lax.axis_size("expert")
    sections = lax.axis_size("section")
    cap_slots = min(row_count, row_count * top_k // experts + 1)
    slot_rows = experts * cap_slots
    hidden = w_gate.shape[-1]
    section_pos = lax.axis_index("section")
    weight_gate = w_gate[0, 0]
    weight_up = w_up[0, 0]
    weight_down = w_down[0, 0]
    route_all = routes[0]
    prob_all = gate_probs[0]
    steps_total = micro_count + sections - 1

    def expert_forward(portion):
        leading = portion.shape[:-1]
        rows_flat = portion.reshape(-1, model_width)
        pre_gate = jnp.dot(rows_flat, weight_gate, preferred_element_type=jnp.float32)
        pre_up = jnp.dot(rows_flat, weight_up, preferred_element_type=jnp.float32)
        activation = (jax.nn.silu(pre_gate) * pre_up).astype(jnp.bfloat16)
        produced = jnp.dot(activation, weight_down, preferred_element_type=jnp.float32).astype(
            jnp.bfloat16
        )
        return (
            portion,
            pre_gate.reshape(leading + (hidden,)),
            pre_up.reshape(leading + (hidden,)),
            produced.reshape(portion.shape),
        )

    def forward_step(step_num, carried):
        incoming, keep_x, keep_rows, keep_gate, keep_up = carried
        micro_pos = step_num - section_pos
        is_live = (micro_pos >= 0) & (micro_pos < micro_count)
        position = jnp.clip(micro_pos, 0, micro_count - 1)
        fresh = lax.dynamic_index_in_dim(tokens, position, 0, keepdims=False)
        current = jnp.where(section_pos == 0, fresh, incoming)
        current_f = current.astype(jnp.float32)
        normed = (current_f * inverse_rms(current_f)).astype(jnp.bfloat16)
        route_ids = lax.dynamic_index_in_dim(route_all, position, 0, keepdims=False)
        probs = lax.dynamic_index_in_dim(prob_all, position, 0, keepdims=False)
        selector = slot_selector(route_ids, experts, cap_slots)
        outgoing = jnp.einsum(
            "rkj,rd->jd", selector, normed, preferred_element_type=jnp.float32
        ).astype(jnp.bfloat16)
        outgoing = outgoing.reshape(experts, cap_slots, model_width)
        received, pre_gate, pre_up, produced = expert_forward(
            lax.all_to_all(outgoing, "expert", split_axis=0, concat_axis=0, tiled=True)
        )
        returned = lax.all_to_all(produced, "expert", split_axis=0, concat_axis=0, tiled=True)
        chosen = jnp.einsum(
            "rkj,jd->rkd",
            selector,
            returned.reshape(slot_rows, model_width),
            preferred_element_type=jnp.float32,
        )
        mixed = (current_f + jnp.einsum("rk,rkd->rd", probs, chosen)).astype(jnp.bfloat16)
        keep_x = keep_entry(keep_x, current, position, is_live)
        keep_rows = keep_entry(
            keep_rows, received.reshape(slot_rows, model_width), position, is_live
        )
        keep_gate = keep_entry(keep_gate, pre_gate.reshape(slot_rows, hidden), position, is_live)
        keep_up = keep_entry(keep_up, pre_up.reshape(slot_rows, hidden), position, is_live)
        incoming = shifted(mixed, "section", 1)
        return (incoming, keep_x, keep_rows, keep_gate, keep_up)

    start_forward = (
        jnp.zeros((row_count, model_width), jnp.bfloat16),
        jnp.zeros((micro_count, row_count, model_width), jnp.bfloat16),
        jnp.zeros((micro_count, slot_rows, model_width), jnp.bfloat16),
        jnp.zeros((micro_count, slot_rows, hidden), jnp.float32),
        jnp.zeros((micro_count, slot_rows, hidden), jnp.float32),
    )
    finished = lax.fori_loop(0, steps_total, forward_step, start_forward)
    keep_x, keep_rows, keep_gate, keep_up = (finished[1], finished[2], finished[3], finished[4])

    def local_backward(operands):
        arrived, pre_gate, pre_up = operands
        back_hidden = lax.dot_general(
            arrived, weight_down, contract_cols, preferred_element_type=jnp.float32
        )
        sigmoid_gate = jax.nn.sigmoid(pre_gate)
        silu_gate = pre_gate * sigmoid_gate
        d_gate = (
            back_hidden * pre_up * sigmoid_gate * (1.0 + pre_gate * (1.0 - sigmoid_gate))
        ).astype(jnp.bfloat16)
        d_up = (back_hidden * silu_gate).astype(jnp.bfloat16)
        activation = (silu_gate * pre_up).astype(jnp.bfloat16)
        d_rows = (
            lax.dot_general(d_gate, weight_gate, contract_cols, preferred_element_type=jnp.float32)
            + lax.dot_general(d_up, weight_up, contract_cols, preferred_element_type=jnp.float32)
        ).astype(jnp.bfloat16)
        return (d_gate, d_up, activation, d_rows)

    def backward_step(step_num, carried):
        incoming, keep_go, keep_dgate, keep_dup, keep_act = carried
        micro_pos = step_num - (sections - 1 - section_pos)
        is_live = (micro_pos >= 0) & (micro_pos < micro_count)
        position = jnp.clip(micro_pos, 0, micro_count - 1)
        given_grad = lax.dynamic_index_in_dim(cotangent, position, 0, keepdims=False)
        upstream = jnp.where(section_pos == sections - 1, given_grad, incoming)
        upstream = jnp.where(is_live, upstream, jnp.zeros_like(upstream))
        upstream_f = upstream.astype(jnp.float32)
        current_f = lax.dynamic_index_in_dim(keep_x, position, 0, keepdims=False).astype(
            jnp.float32
        )
        route_ids = lax.dynamic_index_in_dim(route_all, position, 0, keepdims=False)
        probs = lax.dynamic_index_in_dim(prob_all, position, 0, keepdims=False)
        selector = slot_selector(route_ids, experts, cap_slots)
        scaled = (probs[:, :, None] * upstream_f[:, None, :]).astype(jnp.bfloat16)
        outgoing = jnp.einsum(
            "rkj,rkd->jd", selector, scaled, preferred_element_type=jnp.float32
        ).astype(jnp.bfloat16)
        arrived = lax.all_to_all(
            outgoing.reshape(experts, cap_slots, model_width),
            "expert",
            split_axis=0,
            concat_axis=0,
            tiled=True,
        )
        arrived = arrived.reshape(slot_rows, model_width)
        pre_gate = lax.dynamic_index_in_dim(keep_gate, position, 0, keepdims=False)
        pre_up = lax.dynamic_index_in_dim(keep_up, position, 0, keepdims=False)
        d_gate, d_up, activation, d_rows = local_backward((arrived, pre_gate, pre_up))
        sent_back = lax.all_to_all(
            d_rows.reshape(experts, cap_slots, model_width),
            "expert",
            split_axis=0,
            concat_axis=0,
            tiled=True,
        )
        d_normed = jnp.einsum(
            "rkj,jd->rd",
            selector,
            sent_back.reshape(slot_rows, model_width),
            preferred_element_type=jnp.float32,
        )
        scale_rms = inverse_rms(current_f)
        d_current = scale_rms * d_normed - current_f * scale_rms**3 * jnp.mean(
            d_normed * current_f, -1, keepdims=True
        )
        passed = (upstream_f + d_current).astype(jnp.bfloat16)
        keep_go = keep_entry(keep_go, arrived, position, is_live)
        keep_dgate = keep_entry(keep_dgate, d_gate, position, is_live)
        keep_dup = keep_entry(keep_dup, d_up, position, is_live)
        keep_act = keep_entry(keep_act, activation, position, is_live)
        incoming = shifted(passed, "section", -1)
        return (incoming, keep_go, keep_dgate, keep_dup, keep_act)

    start_backward = (
        jnp.zeros((row_count, model_width), jnp.bfloat16),
        jnp.zeros((micro_count, slot_rows, model_width), jnp.bfloat16),
        jnp.zeros((micro_count, slot_rows, hidden), jnp.bfloat16),
        jnp.zeros((micro_count, slot_rows, hidden), jnp.bfloat16),
        jnp.zeros((micro_count, slot_rows, hidden), jnp.bfloat16),
    )
    done = lax.fori_loop(0, steps_total, backward_step, start_backward)
    all_rows = micro_count * slot_rows
    rows_all = keep_rows.reshape(all_rows, model_width)
    go_all = done[1].reshape(all_rows, model_width)
    dgate_all = done[2].reshape(all_rows, hidden)
    dup_all = done[3].reshape(all_rows, hidden)
    act_all = done[4].reshape(all_rows, hidden)
    rows_part, go_part = (
        lax.all_to_all(rows_all, "dp", split_axis=1, concat_axis=0, tiled=True),
        lax.all_to_all(go_all, "dp", split_axis=1, concat_axis=0, tiled=True),
    )
    dgate_whole, dup_whole, act_whole = (
        lax.all_gather(dgate_all, "dp", axis=0, tiled=True),
        lax.all_gather(dup_all, "dp", axis=0, tiled=True),
        lax.all_gather(act_all, "dp", axis=0, tiled=True),
    )
    grad_gate = lax.dot_general(
        rows_part, dgate_whole, contract_rows, preferred_element_type=jnp.float32
    )
    grad_up = lax.dot_general(
        rows_part, dup_whole, contract_rows, preferred_element_type=jnp.float32
    )
    grad_down = lax.dot_general(
        act_whole, go_part, contract_rows, preferred_element_type=jnp.float32
    )
    return (grad_gate[None, None], grad_up[None, None], grad_down[None, None])


def solution(mesh):
    in_specs = (
        P(None, ("expert", "dp"), None),
        P("section", None, ("expert", "dp"), None),
        P("section", None, ("expert", "dp"), None),
        P("section", "expert", None, None),
        P("section", "expert", None, None),
        P("section", "expert", None, None),
        P(None, ("expert", "dp"), None),
    )
    out_specs = (
        P("section", "expert", "dp", None),
        P("section", "expert", "dp", None),
        P("section", "expert", None, "dp"),
    )
    return jax.shard_map(shards, mesh=mesh, in_specs=in_specs, out_specs=out_specs, check_vma=False)
```

profile of v0, /device:TPU:0, one launch (start us, length us, event | category | flops | bytes accessed | tf_op | source)
XLA Modules:
  0.0 650.3 jit_solution(5906262244409063740)
XLA Ops:
  5.2 266.9 %while.45 = (s32[]{:T(128)}, bf16[32,2048]{1,0:T(8,128)(2,1)S(1)}, bf16[4,32,2048]{2,1,0:T(8,128)(2,1)}, bf16[4,72,2048]{2,1,0:T(8,128)(2,1)}, f32[4,72,640]{2,1...) while((s32[]{:T(128)}, bf16[32,2048]{1,0:T(8,128)(2,1)S(1)}, ...), condition=%wide.region_5.6_spmd, body=%wide.region_0.5_spmd.sunk | while | flops 596245888 | bytes 43867772 | solution.py:112
  10.4 7.3 %all-to-all-start = ((bf16[8,9,2048]{2,1,0:T(8,128)(2,1)}), bf16[8,9,2048]{2,1,0:T(8,128)(2,1)S(1)}, u32[]{:S(2)}, u32[]{:S(2)}) async-start(bf16[8,9,2048]{2,1,0:T(8,128)(2,1)} %reshape.231), calls=%async_computation | async-start | bytes 1048576 | tf_op jit(solution)/shard_map/while/body/eval_jaxpr/all_to_all | solution.py:86
  19.5 12.7 %all-to-all-done = bf16[8,9,2048]{2,1,0:T(8,128)(2,1)S(1)} async-done(((bf16[8,9,2048]{2,1,0:T(8,128)(2,1)}), bf16[8,9,2048]{2,1,0:T(8,128)(2,1)S(1)}, u32[]{:S(2)}, u32[]{:S(2)}) %all-to-all-start) | async-done | bytes 294944 | tf_op jit(solution)/shard_map/while/body/eval_jaxpr/all_to_all | solution.py:86
  38.0 4.1 all-to-all-start.1
  42.5 14.0 %all-to-all-done.1 = bf16[8,9,2048]{2,1,0:T(8,128)(2,1)} async-done(((bf16[8,9,2048]{2,1,0:T(8,128)(2,1)}), bf16[8,9,2048]{2,1,0:T(8,128)(2,1)}, u32[]{:S(2)}, u32[]{:S(2)}) %all-to-all-start.1) | async-done | bytes 294944 | tf_op jit(solution)/shard_map/while/body/eval_jaxpr/all_to_all | solution.py:88
  72.7 12.5 %all-to-all-done = bf16[8,9,2048]{2,1,0:T(8,128)(2,1)S(1)} async-done(((bf16[8,9,2048]{2,1,0:T(8,128)(2,1)}), bf16[8,9,2048]{2,1,0:T(8,128)(2,1)S(1)}, u32[]{:S(2)}, u32[]{:S(2)}) %all-to-all-start) | async-done | bytes 294944 | tf_op jit(solution)/shard_map/while/body/eval_jaxpr/all_to_all | solution.py:86
  90.9 4.1 all-to-all-start.1
  95.4 13.8 %all-to-all-done.1 = bf16[8,9,2048]{2,1,0:T(8,128)(2,1)} async-done(((bf16[8,9,2048]{2,1,0:T(8,128)(2,1)}), bf16[8,9,2048]{2,1,0:T(8,128)(2,1)}, u32[]{:S(2)}, u32[]{:S(2)}) %all-to-all-start.1) | async-done | bytes 294944 | tf_op jit(solution)/shard_map/while/body/eval_jaxpr/all_to_all | solution.py:88
  125.3 12.4 %all-to-all-done = bf16[8,9,2048]{2,1,0:T(8,128)(2,1)S(1)} async-done(((bf16[8,9,2048]{2,1,0:T(8,128)(2,1)}), bf16[8,9,2048]{2,1,0:T(8,128)(2,1)S(1)}, u32[]{:S(2)}, u32[]{:S(2)}) %all-to-all-start) | async-done | bytes 294944 | tf_op jit(solution)/shard_map/while/body/eval_jaxpr/all_to_all | solution.py:86
  143.6 4.1 all-to-all-start.1
  148.0 13.8 %all-to-all-done.1 = bf16[8,9,2048]{2,1,0:T(8,128)(2,1)} async-done(((bf16[8,9,2048]{2,1,0:T(8,128)(2,1)}), bf16[8,9,2048]{2,1,0:T(8,128)(2,1)}, u32[]{:S(2)}, u32[]{:S(2)}) %all-to-all-start.1) | async-done | bytes 294944 | tf_op jit(solution)/shard_map/while/body/eval_jaxpr/all_to_all | solution.py:88
  177.9 12.5 %all-to-all-done = bf16[8,9,2048]{2,1,0:T(8,128)(2,1)S(1)} async-done(((bf16[8,9,2048]{2,1,0:T(8,128)(2,1)}), bf16[8,9,2048]{2,1,0:T(8,128)(2,1)S(1)}, u32[]{:S(2)}, u32[]{:S(2)}) %all-to-all-start) | async-done | bytes 294944 | tf_op jit(solution)/shard_map/while/body/eval_jaxpr/all_to_all | solution.py:86
  196.1 4.1 all-to-all-start.1
  200.6 13.8 %all-to-all-done.1 = bf16[8,9,2048]{2,1,0:T(8,128)(2,1)} async-done(((bf16[8,9,2048]{2,1,0:T(8,128)(2,1)}), bf16[8,9,2048]{2,1,0:T(8,128)(2,1)}, u32[]{:S(2)}, u32[]{:S(2)}) %all-to-all-start.1) | async-done | bytes 294944 | tf_op jit(solution)/shard_map/while/body/eval_jaxpr/all_to_all | solution.py:88
  230.5 12.5 %all-to-all-done = bf16[8,9,2048]{2,1,0:T(8,128)(2,1)S(1)} async-done(((bf16[8,9,2048]{2,1,0:T(8,128)(2,1)}), bf16[8,9,2048]{2,1,0:T(8,128)(2,1)S(1)}, u32[]{:S(2)}, u32[]{:S(2)}) %all-to-all-start) | async-done | bytes 294944 | tf_op jit(solution)/shard_map/while/body/eval_jaxpr/all_to_all | solution.py:86
  248.8 4.1 all-to-all-start.1
  253.2 13.8 %all-to-all-done.1 = bf16[8,9,2048]{2,1,0:T(8,128)(2,1)} async-done(((bf16[8,9,2048]{2,1,0:T(8,128)(2,1)}), bf16[8,9,2048]{2,1,0:T(8,128)(2,1)}, u32[]{:S(2)}, u32[]{:S(2)}) %all-to-all-start.1) | async-done | bytes 294944 | tf_op jit(solution)/shard_map/while/body/eval_jaxpr/all_to_all | solution.py:88
  282.1 290.7 %while.46 = (s32[]{:T(128)}, bf16[32,2048]{1,0:T(8,128)(2,1)S(1)}, bf16[4,72,2048]{2,1,0:T(8,128)(2,1)}, bf16[4,72,640]{2,1,0:T(8,128)(2,1)}, bf16[4,72,640]{2,1...) while((s32[]{:T(128)}, bf16[32,2048]{1,0:T(8,128)(2,1)S(1)}, ...), condition=%wide.region_12.13_spmd, body=%wide.region_6.12_spmd.sunk | while | flops 597448064 | bytes 32585148 | solution.py:195
  291.3 12.7 %all-to-all-done.2 = bf16[8,9,2048]{2,1,0:T(8,128)(2,1)S(1)} async-done(((bf16[8,9,2048]{2,1,0:T(8,128)(2,1)}), bf16[8,9,2048]{2,1,0:T(8,128)(2,1)S(1)}, u32[]{:S(2)}, u32[]{:S(2)}) %all-to-all-start.2) | async-done | bytes 294944 | tf_op jit(solution)/shard_map/while/body/eval_jaxpr/all_to_all | solution.py:152
  318.9 13.2 %all-to-all-done.3 = bf16[8,9,2048]{2,1,0:T(8,128)(2,1)} async-done(((bf16[8,9,2048]{2,1,0:T(8,128)(2,1)}), bf16[8,9,2048]{2,1,0:T(8,128)(2,1)}, u32[]{:S(2)}, u32[]{:S(2)}) %all-to-all-start.3) | async-done | bytes 294944 | tf_op jit(solution)/shard_map/while/body/eval_jaxpr/all_to_all | solution.py:163
  347.6 14.2 %all-to-all-done.2 = bf16[8,9,2048]{2,1,0:T(8,128)(2,1)S(1)} async-done(((bf16[8,9,2048]{2,1,0:T(8,128)(2,1)}), bf16[8,9,2048]{2,1,0:T(8,128)(2,1)S(1)}, u32[]{:S(2)}, u32[]{:S(2)}) %all-to-all-start.2) | async-done | bytes 294944 | tf_op jit(solution)/shard_map/while/body/eval_jaxpr/all_to_all | solution.py:152
  376.6 13.9 %all-to-all-done.3 = bf16[8,9,2048]{2,1,0:T(8,128)(2,1)} async-done(((bf16[8,9,2048]{2,1,0:T(8,128)(2,1)}), bf16[8,9,2048]{2,1,0:T(8,128)(2,1)}, u32[]{:S(2)}, u32[]{:S(2)}) %all-to-all-start.3) | async-done | bytes 294944 | tf_op jit(solution)/shard_map/while/body/eval_jaxpr/all_to_all | solution.py:163
  406.1 14.2 %all-to-all-done.2 = bf16[8,9,2048]{2,1,0:T(8,128)(2,1)S(1)} async-done(((bf16[8,9,2048]{2,1,0:T(8,128)(2,1)}), bf16[8,9,2048]{2,1,0:T(8,128)(2,1)S(1)}, u32[]{:S(2)}, u32[]{:S(2)}) %all-to-all-start.2) | async-done | bytes 294944 | tf_op jit(solution)/shard_map/while/body/eval_jaxpr/all_to_all | solution.py:152
  435.1 13.9 %all-to-all-done.3 = bf16[8,9,2048]{2,1,0:T(8,128)(2,1)} async-done(((bf16[8,9,2048]{2,1,0:T(8,128)(2,1)}), bf16[8,9,2048]{2,1,0:T(8,128)(2,1)}, u32[]{:S(2)}, u32[]{:S(2)}) %all-to-all-start.3) | async-done | bytes 294944 | tf_op jit(solution)/shard_map/while/body/eval_jaxpr/all_to_all | solution.py:163
  464.6 14.2 %all-to-all-done.2 = bf16[8,9,2048]{2,1,0:T(8,128)(2,1)S(1)} async-done(((bf16[8,9,2048]{2,1,0:T(8,128)(2,1)}), bf16[8,9,2048]{2,1,0:T(8,128)(2,1)S(1)}, u32[]{:S(2)}, u32[]{:S(2)}) %all-to-all-start.2) | async-done | bytes 294944 | tf_op jit(solution)/shard_map/while/body/eval_jaxpr/all_to_all | solution.py:152
  493.7 13.9 %all-to-all-done.3 = bf16[8,9,2048]{2,1,0:T(8,128)(2,1)} async-done(((bf16[8,9,2048]{2,1,0:T(8,128)(2,1)}), bf16[8,9,2048]{2,1,0:T(8,128)(2,1)}, u32[]{:S(2)}, u32[]{:S(2)}) %all-to-all-start.3) | async-done | bytes 294944 | tf_op jit(solution)/shard_map/while/body/eval_jaxpr/all_to_all | solution.py:163
  523.1 14.2 %all-to-all-done.2 = bf16[8,9,2048]{2,1,0:T(8,128)(2,1)S(1)} async-done(((bf16[8,9,2048]{2,1,0:T(8,128)(2,1)}), bf16[8,9,2048]{2,1,0:T(8,128)(2,1)S(1)}, u32[]{:S(2)}, u32[]{:S(2)}) %all-to-all-start.2) | async-done | bytes 294944 | tf_op jit(solution)/shard_map/while/body/eval_jaxpr/all_to_all | solution.py:152
  552.3 13.9 %all-to-all-done.3 = bf16[8,9,2048]{2,1,0:T(8,128)(2,1)} async-done(((bf16[8,9,2048]{2,1,0:T(8,128)(2,1)}), bf16[8,9,2048]{2,1,0:T(8,128)(2,1)}, u32[]{:S(2)}, u32[]{:S(2)}) %all-to-all-start.3) | async-done | bytes 294944 | tf_op jit(solution)/shard_map/while/body/eval_jaxpr/all_to_all | solution.py:163
  572.9 4.6 all-to-all-start.4
  579.8 22.0 %all_gather.11 = bf16[576,640]{1,0:T(8,128)(2,1)S(1)} all-gather(bf16[288,640]{1,0:T(8,128)(2,1)S(1)} %bitcast.206), channel_id=1, replica_groups=mesh['section'=2,'expert'=8,'dp'=2] {'dp'}, dimensions={0}, use_global_device_ids=true | all-gather | bytes 1105920 | tf_op jit(solution)/shard_map/all_gather | solution.py:209
  601.7 11.2 %all_gather.10 = bf16[576,640]{1,0:T(8,128)(2,1)S(1)} all-gather(bf16[288,640]{1,0:T(8,128)(2,1)S(1)} %bitcast.204), channel_id=1, replica_groups=mesh['section'=2,'expert'=8,'dp'=2] {'dp'}, dimensions={0}, use_global_device_ids=true | all-gather | bytes 1105920 | tf_op jit(solution)/shard_map/all_gather | solution.py:208
  616.7 22.6 %all_gather.9 = bf16[576,640]{1,0:T(8,128)(2,1)S(1)} all-gather(bf16[288,640]{1,0:T(8,128)(2,1)S(1)} %bitcast.205), channel_id=1, replica_groups=mesh['section'=2,'expert'=8,'dp'=2] {'dp'}, dimensions={0}, use_global_device_ids=true | all-gather | bytes 1105920 | tf_op jit(solution)/shard_map/all_gather | solution.py:207
  (422 shorter events, 289.9 us)
Async XLA Ops:
  10.4 21.8 %all-to-all-start = ((bf16[8,9,2048]{2,1,0:T(8,128)(2,1)}), bf16[8,9,2048]{2,1,0:T(8,128)(2,1)S(1)}, u32[]{:S(2)}, u32[]{:S(2)}) async-start(bf16[8,9,2048]{2,1,0:T(8,128)(2,1)} %reshape.231), calls=%async_computation | async-start | bytes 1048576 | tf_op jit(solution)/shard_map/while/body/eval_jaxpr/all_to_all | solution.py:86
  38.0 18.4 %all-to-all-start.1 = ((bf16[8,9,2048]{2,1,0:T(8,128)(2,1)}), bf16[8,9,2048]{2,1,0:T(8,128)(2,1)}, u32[]{:S(2)}, u32[]{:S(2)}) async-start(bf16[8,9,2048]{2,1,0:T(8,128)(2,1)} %reshape.233), calls=%async_computation.1 | async-start | bytes 1048576 | tf_op jit(solution)/shard_map/while/body/eval_jaxpr/all_to_all | solution.py:88
  58.4 3.1 collective-permute-start
  66.7 18.4 %all-to-all-start = ((bf16[8,9,2048]{2,1,0:T(8,128)(2,1)}), bf16[8,9,2048]{2,1,0:T(8,128)(2,1)S(1)}, u32[]{:S(2)}, u32[]{:S(2)}) async-start(bf16[8,9,2048]{2,1,0:T(8,128)(2,1)} %reshape.231), calls=%async_computation | async-start | bytes 1048576 | tf_op jit(solution)/shard_map/while/body/eval_jaxpr/all_to_all | solution.py:86
  90.9 18.3 %all-to-all-start.1 = ((bf16[8,9,2048]{2,1,0:T(8,128)(2,1)}), bf16[8,9,2048]{2,1,0:T(8,128)(2,1)}, u32[]{:S(2)}, u32[]{:S(2)}) async-start(bf16[8,9,2048]{2,1,0:T(8,128)(2,1)} %reshape.233), calls=%async_computation.1 | async-start | bytes 1048576 | tf_op jit(solution)/shard_map/while/body/eval_jaxpr/all_to_all | solution.py:88
  111.2 3.1 collective-permute-start
  119.5 18.2 %all-to-all-start = ((bf16[8,9,2048]{2,1,0:T(8,128)(2,1)}), bf16[8,9,2048]{2,1,0:T(8,128)(2,1)S(1)}, u32[]{:S(2)}, u32[]{:S(2)}) async-start(bf16[8,9,2048]{2,1,0:T(8,128)(2,1)} %reshape.231), calls=%async_computation | async-start | bytes 1048576 | tf_op jit(solution)/shard_map/while/body/eval_jaxpr/all_to_all | solution.py:86
  143.6 18.2 %all-to-all-start.1 = ((bf16[8,9,2048]{2,1,0:T(8,128)(2,1)}), bf16[8,9,2048]{2,1,0:T(8,128)(2,1)}, u32[]{:S(2)}, u32[]{:S(2)}) async-start(bf16[8,9,2048]{2,1,0:T(8,128)(2,1)} %reshape.233), calls=%async_computation.1 | async-start | bytes 1048576 | tf_op jit(solution)/shard_map/while/body/eval_jaxpr/all_to_all | solution.py:88
  163.8 3.1 collective-permute-start
  172.1 18.2 %all-to-all-start = ((bf16[8,9,2048]{2,1,0:T(8,128)(2,1)}), bf16[8,9,2048]{2,1,0:T(8,128)(2,1)S(1)}, u32[]{:S(2)}, u32[]{:S(2)}) async-start(bf16[8,9,2048]{2,1,0:T(8,128)(2,1)} %reshape.231), calls=%async_computation | async-start | bytes 1048576 | tf_op jit(solution)/shard_map/while/body/eval_jaxpr/all_to_all | solution.py:86
  196.1 18.3 %all-to-all-start.1 = ((bf16[8,9,2048]{2,1,0:T(8,128)(2,1)}), bf16[8,9,2048]{2,1,0:T(8,128)(2,1)}, u32[]{:S(2)}, u32[]{:S(2)}) async-start(bf16[8,9,2048]{2,1,0:T(8,128)(2,1)} %reshape.233), calls=%async_computation.1 | async-start | bytes 1048576 | tf_op jit(solution)/shard_map/while/body/eval_jaxpr/all_to_all | solution.py:88
  216.4 3.1 collective-permute-start
  224.7 18.2 %all-to-all-start = ((bf16[8,9,2048]{2,1,0:T(8,128)(2,1)}), bf16[8,9,2048]{2,1,0:T(8,128)(2,1)S(1)}, u32[]{:S(2)}, u32[]{:S(2)}) async-start(bf16[8,9,2048]{2,1,0:T(8,128)(2,1)} %reshape.231), calls=%async_computation | async-start | bytes 1048576 | tf_op jit(solution)/shard_map/while/body/eval_jaxpr/all_to_all | solution.py:86
  248.8 18.3 %all-to-all-start.1 = ((bf16[8,9,2048]{2,1,0:T(8,128)(2,1)}), bf16[8,9,2048]{2,1,0:T(8,128)(2,1)}, u32[]{:S(2)}, u32[]{:S(2)}) async-start(bf16[8,9,2048]{2,1,0:T(8,128)(2,1)} %reshape.233), calls=%async_computation.1 | async-start | bytes 1048576 | tf_op jit(solution)/shard_map/while/body/eval_jaxpr/all_to_all | solution.py:88
  269.0 3.1 collective-permute-start
  285.8 18.2 %all-to-all-start.2 = ((bf16[8,9,2048]{2,1,0:T(8,128)(2,1)}), bf16[8,9,2048]{2,1,0:T(8,128)(2,1)S(1)}, u32[]{:S(2)}, u32[]{:S(2)}) async-start(bf16[8,9,2048]{2,1,0:T(8,128)(2,1)} %reshape.236), calls=%async_computation.2 | async-start | bytes 1048576 | tf_op jit(solution)/shard_map/while/body/eval_jaxpr/all_to_all | solution.py:152
  313.8 18.2 %all-to-all-start.3 = ((bf16[8,9,2048]{2,1,0:T(8,128)(2,1)}), bf16[8,9,2048]{2,1,0:T(8,128)(2,1)}, u32[]{:S(2)}, u32[]{:S(2)}) async-start(bf16[8,9,2048]{2,1,0:T(8,128)(2,1)} %reshape.238), calls=%async_computation.3 | async-start | bytes 1048576 | tf_op jit(solution)/shard_map/while/body/eval_jaxpr/all_to_all | solution.py:163
  335.5 3.2 collective-permute-start.1
  342.4 19.4 %all-to-all-start.2 = ((bf16[8,9,2048]{2,1,0:T(8,128)(2,1)}), bf16[8,9,2048]{2,1,0:T(8,128)(2,1)S(1)}, u32[]{:S(2)}, u32[]{:S(2)}) async-start(bf16[8,9,2048]{2,1,0:T(8,128)(2,1)} %reshape.236), calls=%async_computation.2 | async-start | bytes 1048576 | tf_op jit(solution)/shard_map/while/body/eval_jaxpr/all_to_all | solution.py:152
  371.6 18.9 %all-to-all-start.3 = ((bf16[8,9,2048]{2,1,0:T(8,128)(2,1)}), bf16[8,9,2048]{2,1,0:T(8,128)(2,1)}, u32[]{:S(2)}, u32[]{:S(2)}) async-start(bf16[8,9,2048]{2,1,0:T(8,128)(2,1)} %reshape.238), calls=%async_computation.3 | async-start | bytes 1048576 | tf_op jit(solution)/shard_map/while/body/eval_jaxpr/all_to_all | solution.py:163
  394.0 3.2 collective-permute-start.1
  400.9 19.4 %all-to-all-start.2 = ((bf16[8,9,2048]{2,1,0:T(8,128)(2,1)}), bf16[8,9,2048]{2,1,0:T(8,128)(2,1)S(1)}, u32[]{:S(2)}, u32[]{:S(2)}) async-start(bf16[8,9,2048]{2,1,0:T(8,128)(2,1)} %reshape.236), calls=%async_computation.2 | async-start | bytes 1048576 | tf_op jit(solution)/shard_map/while/body/eval_jaxpr/all_to_all | solution.py:152
  430.1 19.0 %all-to-all-start.3 = ((bf16[8,9,2048]{2,1,0:T(8,128)(2,1)}), bf16[8,9,2048]{2,1,0:T(8,128)(2,1)}, u32[]{:S(2)}, u32[]{:S(2)}) async-start(bf16[8,9,2048]{2,1,0:T(8,128)(2,1)} %reshape.238), calls=%async_computation.3 | async-start | bytes 1048576 | tf_op jit(solution)/shard_map/while/body/eval_jaxpr/all_to_all | solution.py:163
  452.5 3.2 collective-permute-start.1
  459.4 19.4 %all-to-all-start.2 = ((bf16[8,9,2048]{2,1,0:T(8,128)(2,1)}), bf16[8,9,2048]{2,1,0:T(8,128)(2,1)S(1)}, u32[]{:S(2)}, u32[]{:S(2)}) async-start(bf16[8,9,2048]{2,1,0:T(8,128)(2,1)} %reshape.236), calls=%async_computation.2 | async-start | bytes 1048576 | tf_op jit(solution)/shard_map/while/body/eval_jaxpr/all_to_all | solution.py:152
  488.6 19.0 %all-to-all-start.3 = ((bf16[8,9,2048]{2,1,0:T(8,128)(2,1)}), bf16[8,9,2048]{2,1,0:T(8,128)(2,1)}, u32[]{:S(2)}, u32[]{:S(2)}) async-start(bf16[8,9,2048]{2,1,0:T(8,128)(2,1)} %reshape.238), calls=%async_computation.3 | async-start | bytes 1048576 | tf_op jit(solution)/shard_map/while/body/eval_jaxpr/all_to_all | solution.py:163
  511.1 3.2 collective-permute-start.1
  518.0 19.4 %all-to-all-start.2 = ((bf16[8,9,2048]{2,1,0:T(8,128)(2,1)}), bf16[8,9,2048]{2,1,0:T(8,128)(2,1)S(1)}, u32[]{:S(2)}, u32[]{:S(2)}) async-start(bf16[8,9,2048]{2,1,0:T(8,128)(2,1)} %reshape.236), calls=%async_computation.2 | async-start | bytes 1048576 | tf_op jit(solution)/shard_map/while/body/eval_jaxpr/all_to_all | solution.py:152
  547.2 19.0 %all-to-all-start.3 = ((bf16[8,9,2048]{2,1,0:T(8,128)(2,1)}), bf16[8,9,2048]{2,1,0:T(8,128)(2,1)}, u32[]{:S(2)}, u32[]{:S(2)}) async-start(bf16[8,9,2048]{2,1,0:T(8,128)(2,1)} %reshape.238), calls=%async_computation.3 | async-start | bytes 1048576 | tf_op jit(solution)/shard_map/while/body/eval_jaxpr/all_to_all | solution.py:163
  569.6 3.2 collective-permute-start.1
  572.9 40.1 %all-to-all-start.4 = ((bf16[288,2,1024]{2,0,1:T(8,128)(2,1)}), bf16[288,2,1024]{2,0,1:T(8,128)(2,1)}, u32[]{:S(2)}, u32[]{:S(2)}) async-start(bf16[288,2,1024]{2,0,1:T(8,128)(2,1)} %copy.40), calls=%async_computation.4 | async-start | bytes 2359296 | tf_op jit(solution)/shard_map/all_to_all | solution.py:203
  613.0 34.6 %all-to-all-start.5 = ((bf16[288,2,1024]{2,0,1:T(8,128)(2,1)}), bf16[288,2,1024]{2,0,1:T(8,128)(2,1)S(1)}, u32[]{:S(2)}, u32[]{:S(2)}) async-start(bf16[288,2,1024]{2,0,1:T(8,128)(2,1)} %copy.41), calls=%async_computation.5 | async-start | bytes 2359296 | tf_op jit(solution)/shard_map/all_to_all | solution.py:204
  (41 other events, 254.8 us)
where the time goes:
time: 655 us; the launch traced here: 650 us
  waiting for transfers between devices  271 us (41%)
  starting transfers between devices  105 us (16%)
  local copies, waits for them, and re-layouts  99 us (15%)
  matrix products  76.2 us (12%)
  blocking collectives  55.8 us (9%)
  other arithmetic  41.8 us (6%)
    all_to_all x5, waiting for transfers between devices, backward_step(): lax.all_to_all(outgoing.reshape(experts, cap_slots, model_width), 'expert...  69.5 us
    all_to_all x5, waiting for transfers between devices, forward_step(): lax.all_to_all(produced, 'expert', split_axis=0, concat_axis=0, tiled=True)  69.3 us
    all_to_all x5, waiting for transfers between devices, backward_step(): lax.all_to_all(d_rows.reshape(experts, cap_slots, model_width), 'expert',...  68.8 us
    all_to_all x5, waiting for transfers between devices, forward_step(): lax.all_to_all(outgoing, 'expert', split_axis=0, concat_axis=0, tiled=True)  62.5 us
    dynamic_update_slice x15, other arithmetic, keep_entry(): lax.dynamic_update_index_in_dim(store, jnp.where(is_live, value, previous...  25.6 us
    all_to_all x5, starting transfers between devices, forward_step(): lax.all_to_all(outgoing, 'expert', split_axis=0, concat_axis=0, tiled=True)  23.4 us
    all_gather x1, blocking collectives, shards(): lax.all_gather(dgate_all, 'dp', axis=0, tiled=True)  22.6 us
    all_gather x1, blocking collectives, shards(): lax.all_gather(act_all, 'dp', axis=0, tiled=True)  22 us
  transfers between devices with their start and end apart: 32, of which 25 were waited for; matrix products, arithmetic and copies ran while one was open for 8% of the time, Pallas kernels for 0%

commit v1 on v0

--- a/solution.py
+++ b/solution.py
@@ -6,6 +6,21 @@
 epsilon = 1e-05
 contract_rows = (((0,), (0,)), ((), ()))
 contract_cols = (((1,), (1,)), ((), ()))
+
+
+def _supply_racks(vals, axis_k, patch):
+    even, aux = (vals.shape[:axis_k], vals.shape[axis_k + 1 :])
+    e_now = jnp.moveaxis(vals.reshape(*even, patch, -1, *aux), axis_k, 0)
+    return e_now
+
+
+def point_regions(point, where_dim):
+    point = jnp.moveaxis(point, 0, where_dim)
+    out_arr = point.shape
+    h_now = point.reshape(
+        *out_arr[:where_dim], out_arr[where_dim] * out_arr[where_dim + 1], *out_arr[where_dim + 2 :]
+    )
+    return h_now
 
 
 def shifted(value, axis, by):
@@ -82,8 +97,27 @@
             "rkj,rd->jd", selector, normed, preferred_element_type=jnp.float32
         ).astype(jnp.bfloat16)
         outgoing = outgoing.reshape(experts, cap_slots, model_width)
+
+        def note_zone_over_axis(payload, which_axis, v0, my_data):
+            state_next = lax.psum(1, axis_name=which_axis)
+            z2 = lax.axis_index(which_axis)
+            placed, vec_out = (state_next, z2)
+            mixed_arr = _supply_racks(payload, v0, placed)
+            ready = mixed_arr
+            for j0 in range(1, placed):
+                item_now, carry_in = ((vec_out + j0) % placed, (vec_out - j0) % placed)
+                top = lax.dynamic_index_in_dim(mixed_arr, item_now, 0)
+                n_now = lax.ppermute(
+                    top,
+                    axis_name=which_axis,
+                    perm=[(jj, (jj + j0) % placed) for jj in range(placed)],
+                )
+                ready = lax.dynamic_update_slice_in_dim(ready, n_now, carry_in, axis=0)
+            r1 = point_regions(ready, my_data)
+            return r1
+
         received, pre_gate, pre_up, produced = expert_forward(
-            lax.all_to_all(outgoing, "expert", split_axis=0, concat_axis=0, tiled=True)
+            note_zone_over_axis(outgoing, "expert", 0, 0)
         )
         returned = lax.all_to_all(produced, "expert", split_axis=0, concat_axis=0, tiled=True)
         chosen = jnp.einsum(

time: 655 us -> 666 us (1.017)
  starting transfers between devices: 105 us -> 134 us
  waiting for transfers between devices: 271 us -> 248 us
    all_to_all x5 -> x0, waiting for transfers between devices: 62.5 us -> none  [forward_step(): lax.all_to_all(outgoing, 'expert', split_axis=0, concat_axis=0, tiled=True)]
    ppermute x0 -> x35, starting transfers between devices: none -> 50.1 us  [note_zone_over_axis(): lax.ppermute(top, axis_name=which_axis, perm=[(jj, (jj + j0) % placed) fo...]
    ppermute x0 -> x35, waiting for transfers between devices: none -> 46.1 us  [note_zone_over_axis(): lax.ppermute(top, axis_name=which_axis, perm=[(jj, (jj + j0) % placed) fo...]
    all_to_all x5 -> x0, starting transfers between devices: 23.4 us -> none  [forward_step(): lax.all_to_all(outgoing, 'expert', split_axis=0, concat_axis=0, tiled=True)]
    dynamic_slice x0 -> x10, local copies, waits for them, and re-layouts: none -> 7.51 us  [note_zone_over_axis(): top = lax.dynamic_index_in_dim(mixed_arr, item_now, 0)]
  transfers between devices with their start and end apart: 32 -> 62, of which waited for: 25 -> 40; matrix products, arithmetic and copies ran while one was open for 8% -> 8% of each run, Pallas kernels for 0% -> 0%
where the time goes in v1:
time: 666 us; the launch traced here: 662 us
  waiting for transfers between devices  248 us (37%)
  starting transfers between devices  134 us (20%)
  local copies, waits for them, and re-layouts  103 us (15%)
  matrix products  76.4 us (11%)
  blocking collectives  55.8 us (8%)
  other arithmetic  41.9 us (6%)
    all_to_all x5, waiting for transfers between devices, backward_step(): lax.all_to_all(outgoing.reshape(experts, cap_slots, model_width), 'expert...  69.6 us
    all_to_all x5, waiting for transfers between devices, backward_step(): lax.all_to_all(d_rows.reshape(experts, cap_slots, model_width), 'expert',...  68.8 us
    all_to_all x5, waiting for transfers between devices, forward_step(): lax.all_to_all(produced, 'expert', split_axis=0, concat_axis=0, tiled=True)  63.2 us
    ppermute x35, starting transfers between devices, note_zone_over_axis(): lax.ppermute(top, axis_name=which_axis, perm=[(jj, (jj + j0) % placed) fo...  50.1 us
    ppermute x35, waiting for transfers between devices, note_zone_over_axis(): lax.ppermute(top, axis_name=which_axis, perm=[(jj, (jj + j0) % placed) fo...  46.1 us
    dynamic_update_slice x15, other arithmetic, keep_entry(): lax.dynamic_update_index_in_dim(store, jnp.where(is_live, value, previous...  25.6 us
    all_to_all x5, starting transfers between devices, forward_step(): lax.all_to_all(produced, 'expert', split_axis=0, concat_axis=0, tiled=True)  24.1 us
    all_gather x1, blocking collectives, shards(): lax.all_gather(dgate_all, 'dp', axis=0, tiled=True)  22.6 us
  transfers between devices with their start and end apart: 62, of which 40 were waited for; matrix products, arithmetic and copies ran while one was open for 8% of the time, Pallas kernels for 0%

profile of v1, /device:TPU:0, one launch (start us, length us, event | category | flops | bytes accessed | tf_op | source)
XLA Modules:
  0.0 662.0 jit_solution(927160713500338190)
XLA Ops:
  5.2 278.4 %while.46 = (s32[]{:T(128)}, bf16[32,2048]{1,0:T(8,128)(2,1)S(1)}, bf16[4,32,2048]{2,1,0:T(8,128)(2,1)}, bf16[4,72,2048]{2,1,0:T(8,128)(2,1)}, f32[4,72,640]{2,1...) while((s32[]{:T(128)}, bf16[32,2048]{1,0:T(8,128)(2,1)S(1)}, ...), condition=%wide.region_5.6_spmd, body=%wide.region_0.5_spmd.sunk | while | flops 596246080 | bytes 45279384 | solution.py:146
  12.7 5.4 collective-permute-done
  39.2 5.4 all-to-all-start
  44.9 13.3 %all-to-all-done = bf16[8,9,2048]{2,1,0:T(8,128)(2,1)} async-done(((bf16[8,9,2048]{2,1,0:T(8,128)(2,1)}), bf16[8,9,2048]{2,1,0:T(8,128)(2,1)}, u32[]{:S(2)}, u32[]{:S(2)}) %all-to-all-start) | async-done | bytes 294944 | tf_op jit(solution)/shard_map/while/body/eval_jaxpr/all_to_all | solution.py:122
  69.3 5.6 collective-permute-done
  95.9 4.7 all-to-all-start
  100.8 12.5 %all-to-all-done = bf16[8,9,2048]{2,1,0:T(8,128)(2,1)} async-done(((bf16[8,9,2048]{2,1,0:T(8,128)(2,1)}), bf16[8,9,2048]{2,1,0:T(8,128)(2,1)}, u32[]{:S(2)}, u32[]{:S(2)}) %all-to-all-start) | async-done | bytes 294944 | tf_op jit(solution)/shard_map/while/body/eval_jaxpr/all_to_all | solution.py:122
  124.4 5.6 collective-permute-done
  151.0 4.7 all-to-all-start
  155.9 12.4 %all-to-all-done = bf16[8,9,2048]{2,1,0:T(8,128)(2,1)} async-done(((bf16[8,9,2048]{2,1,0:T(8,128)(2,1)}), bf16[8,9,2048]{2,1,0:T(8,128)(2,1)}, u32[]{:S(2)}, u32[]{:S(2)}) %all-to-all-start) | async-done | bytes 294944 | tf_op jit(solution)/shard_map/while/body/eval_jaxpr/all_to_all | solution.py:122
  179.4 5.6 collective-permute-done
  206.1 4.7 all-to-all-start
  211.0 12.4 %all-to-all-done = bf16[8,9,2048]{2,1,0:T(8,128)(2,1)} async-done(((bf16[8,9,2048]{2,1,0:T(8,128)(2,1)}), bf16[8,9,2048]{2,1,0:T(8,128)(2,1)}, u32[]{:S(2)}, u32[]{:S(2)}) %all-to-all-start) | async-done | bytes 294944 | tf_op jit(solution)/shard_map/while/body/eval_jaxpr/all_to_all | solution.py:122
  234.5 5.6 collective-permute-done
  261.1 4.7 all-to-all-start
  266.1 12.4 %all-to-all-done = bf16[8,9,2048]{2,1,0:T(8,128)(2,1)} async-done(((bf16[8,9,2048]{2,1,0:T(8,128)(2,1)}), bf16[8,9,2048]{2,1,0:T(8,128)(2,1)}, u32[]{:S(2)}, u32[]{:S(2)}) %all-to-all-start) | async-done | bytes 294944 | tf_op jit(solution)/shard_map/while/body/eval_jaxpr/all_to_all | solution.py:122
  293.6 290.9 %while.47 = (s32[]{:T(128)}, bf16[32,2048]{1,0:T(8,128)(2,1)S(1)}, bf16[4,72,2048]{2,1,0:T(8,128)(2,1)}, bf16[4,72,640]{2,1,0:T(8,128)(2,1)}, bf16[4,72,640]{2,1...) while((s32[]{:T(128)}, bf16[32,2048]{1,0:T(8,128)(2,1)S(1)}, ...), condition=%wide.region_12.13_spmd, body=%wide.region_6.12_spmd.sunk | while | flops 597448064 | bytes 32585148 | solution.py:229
  302.5 12.7 %all-to-all-done.1 = bf16[8,9,2048]{2,1,0:T(8,128)(2,1)S(1)} async-done(((bf16[8,9,2048]{2,1,0:T(8,128)(2,1)}), bf16[8,9,2048]{2,1,0:T(8,128)(2,1)S(1)}, u32[]{:S(2)}, u32[]{:S(2)}) %all-to-all-start.1) | async-done | bytes 294944 | tf_op jit(solution)/shard_map/while/body/eval_jaxpr/all_to_all | solution.py:186
  330.2 13.2 %all-to-all-done.2 = bf16[8,9,2048]{2,1,0:T(8,128)(2,1)} async-done(((bf16[8,9,2048]{2,1,0:T(8,128)(2,1)}), bf16[8,9,2048]{2,1,0:T(8,128)(2,1)}, u32[]{:S(2)}, u32[]{:S(2)}) %all-to-all-start.2) | async-done | bytes 294944 | tf_op jit(solution)/shard_map/while/body/eval_jaxpr/all_to_all | solution.py:197
  359.0 14.2 %all-to-all-done.1 = bf16[8,9,2048]{2,1,0:T(8,128)(2,1)S(1)} async-done(((bf16[8,9,2048]{2,1,0:T(8,128)(2,1)}), bf16[8,9,2048]{2,1,0:T(8,128)(2,1)S(1)}, u32[]{:S(2)}, u32[]{:S(2)}) %all-to-all-start.1) | async-done | bytes 294944 | tf_op jit(solution)/shard_map/while/body/eval_jaxpr/all_to_all | solution.py:186
  388.1 13.9 %all-to-all-done.2 = bf16[8,9,2048]{2,1,0:T(8,128)(2,1)} async-done(((bf16[8,9,2048]{2,1,0:T(8,128)(2,1)}), bf16[8,9,2048]{2,1,0:T(8,128)(2,1)}, u32[]{:S(2)}, u32[]{:S(2)}) %all-to-all-start.2) | async-done | bytes 294944 | tf_op jit(solution)/shard_map/while/body/eval_jaxpr/all_to_all | solution.py:197
  417.5 14.2 %all-to-all-done.1 = bf16[8,9,2048]{2,1,0:T(8,128)(2,1)S(1)} async-done(((bf16[8,9,2048]{2,1,0:T(8,128)(2,1)}), bf16[8,9,2048]{2,1,0:T(8,128)(2,1)S(1)}, u32[]{:S(2)}, u32[]{:S(2)}) %all-to-all-start.1) | async-done | bytes 294944 | tf_op jit(solution)/shard_map/while/body/eval_jaxpr/all_to_all | solution.py:186
  446.7 13.9 %all-to-all-done.2 = bf16[8,9,2048]{2,1,0:T(8,128)(2,1)} async-done(((bf16[8,9,2048]{2,1,0:T(8,128)(2,1)}), bf16[8,9,2048]{2,1,0:T(8,128)(2,1)}, u32[]{:S(2)}, u32[]{:S(2)}) %all-to-all-start.2) | async-done | bytes 294944 | tf_op jit(solution)/shard_map/while/body/eval_jaxpr/all_to_all | solution.py:197
  476.2 14.2 %all-to-all-done.1 = bf16[8,9,2048]{2,1,0:T(8,128)(2,1)S(1)} async-done(((bf16[8,9,2048]{2,1,0:T(8,128)(2,1)}), bf16[8,9,2048]{2,1,0:T(8,128)(2,1)S(1)}, u32[]{:S(2)}, u32[]{:S(2)}) %all-to-all-start.1) | async-done | bytes 294944 | tf_op jit(solution)/shard_map/while/body/eval_jaxpr/all_to_all | solution.py:186
  500.3 4.1 all-to-all-start.2
  505.3 13.9 %all-to-all-done.2 = bf16[8,9,2048]{2,1,0:T(8,128)(2,1)} async-done(((bf16[8,9,2048]{2,1,0:T(8,128)(2,1)}), bf16[8,9,2048]{2,1,0:T(8,128)(2,1)}, u32[]{:S(2)}, u32[]{:S(2)}) %all-to-all-start.2) | async-done | bytes 294944 | tf_op jit(solution)/shard_map/while/body/eval_jaxpr/all_to_all | solution.py:197
  534.8 14.2 %all-to-all-done.1 = bf16[8,9,2048]{2,1,0:T(8,128)(2,1)S(1)} async-done(((bf16[8,9,2048]{2,1,0:T(8,128)(2,1)}), bf16[8,9,2048]{2,1,0:T(8,128)(2,1)S(1)}, u32[]{:S(2)}, u32[]{:S(2)}) %all-to-all-start.1) | async-done | bytes 294944 | tf_op jit(solution)/shard_map/while/body/eval_jaxpr/all_to_all | solution.py:186
  564.0 13.9 %all-to-all-done.2 = bf16[8,9,2048]{2,1,0:T(8,128)(2,1)} async-done(((bf16[8,9,2048]{2,1,0:T(8,128)(2,1)}), bf16[8,9,2048]{2,1,0:T(8,128)(2,1)}, u32[]{:S(2)}, u32[]{:S(2)}) %all-to-all-start.2) | async-done | bytes 294944 | tf_op jit(solution)/shard_map/while/body/eval_jaxpr/all_to_all | solution.py:197
  584.5 4.6 all-to-all-start.3
  591.4 22.0 %all_gather.11 = bf16[576,640]{1,0:T(8,128)(2,1)S(1)} all-gather(bf16[288,640]{1,0:T(8,128)(2,1)S(1)} %bitcast.210), channel_id=1, replica_groups=mesh['section'=2,'expert'=8,'dp'=2] {'dp'}, dimensions={0}, use_global_device_ids=true | all-gather | bytes 1105920 | tf_op jit(solution)/shard_map/all_gather | solution.py:243
  613.4 11.2 %all_gather.10 = bf16[576,640]{1,0:T(8,128)(2,1)S(1)} all-gather(bf16[288,640]{1,0:T(8,128)(2,1)S(1)} %bitcast.208), channel_id=1, replica_groups=mesh['section'=2,'expert'=8,'dp'=2] {'dp'}, dimensions={0}, use_global_device_ids=true | all-gather | bytes 1105920 | tf_op jit(solution)/shard_map/all_gather | solution.py:242
  628.4 22.6 %all_gather.9 = bf16[576,640]{1,0:T(8,128)(2,1)S(1)} all-gather(bf16[288,640]{1,0:T(8,128)(2,1)S(1)} %bitcast.209), channel_id=1, replica_groups=mesh['section'=2,'expert'=8,'dp'=2] {'dp'}, dimensions={0}, use_global_device_ids=true | all-gather | bytes 1105920 | tf_op jit(solution)/shard_map/all_gather | solution.py:241
  (522 shorter events, 341.7 us)
Async XLA Ops:
  9.7 8.4 %collective-permute-start = (bf16[1,1,9,2048]{3,2,0,1:T(8,128)(2,1)S(1)}, bf16[1,1,9,2048]{3,2,0,1:T(8,128)(2,1)}, u32[]{:S(2)}, u32[]{:S(2)}) collective-permute-start(bf16[1,1,9,2048]{3,2,0,1:T(8,128)(2,1)S(1)} %constant_dynamic-slice_fusion.26), channel_id=1, source_target_pairs={{0,2},{2,4},{4,6},{6,8},{8,10},{10,12},{12,14},{14,0},{1,3},{3,5},... | collective-permute-start | bytes 110600 | tf_op jit(solution)/shard_map/while/body/eval_jaxpr/ppermute | solution.py:110
  19.6 9.5 %collective-permute-start.1 = (bf16[1,1,9,2048]{3,2,0,1:T(8,128)(2,1)}, bf16[1,1,9,2048]{3,2,0,1:T(8,128)(2,1)S(1)}, u32[]{:S(2)}, u32[]{:S(2)}) collective-permute-start(bf16[1,1,9,2048]{3,2,0,1:T(8,128)(2,1)} %get-tuple-element.995), channel_id=1, source_target_pairs={{0,4},{2,6},{4,8},{6,10},{8,12},{10,14},{12,0},{14,2},{1,5},{3,7},... | collective-permute-start | bytes 110600 | tf_op jit(solution)/shard_map/while/body/eval_jaxpr/ppermute | solution.py:110
  21.4 8.2 %collective-permute-start.2 = (bf16[1,1,9,2048]{3,2,0,1:T(8,128)(2,1)S(1)}, bf16[1,1,9,2048]{3,2,0,1:T(8,128)(2,1)S(1)}, u32[]{:S(2)}, u32[]{:S(2)}) collective-permute-start(bf16[1,1,9,2048]{3,2,0,1:T(8,128)(2,1)S(1)} %get-tuple-element.996), channel_id=1, source_target_pairs={{0,6},{2,8},{4,10},{6,12},{8,14},{10,0},{12,2},{14,4},{1,7},{3,9},... | collective-permute-start | bytes 110600 | tf_op jit(solution)/shard_map/while/body/eval_jaxpr/ppermute | solution.py:110
  39.2 19.0 %all-to-all-start = ((bf16[8,9,2048]{2,1,0:T(8,128)(2,1)}), bf16[8,9,2048]{2,1,0:T(8,128)(2,1)}, u32[]{:S(2)}, u32[]{:S(2)}) async-start(bf16[8,9,2048]{2,1,0:T(8,128)(2,1)} %reshape.247), calls=%async_computation | async-start | bytes 1048576 | tf_op jit(solution)/shard_map/while/body/eval_jaxpr/all_to_all | solution.py:122
  76.4 9.4 %collective-permute-start.1 = (bf16[1,1,9,2048]{3,2,0,1:T(8,128)(2,1)}, bf16[1,1,9,2048]{3,2,0,1:T(8,128)(2,1)S(1)}, u32[]{:S(2)}, u32[]{:S(2)}) collective-permute-start(bf16[1,1,9,2048]{3,2,0,1:T(8,128)(2,1)} %get-tuple-element.995), channel_id=1, source_target_pairs={{0,4},{2,6},{4,8},{6,10},{8,12},{10,14},{12,0},{14,2},{1,5},{3,7},... | collective-permute-start | bytes 110600 | tf_op jit(solution)/shard_map/while/body/eval_jaxpr/ppermute | solution.py:110
  78.2 8.2 %collective-permute-start.2 = (bf16[1,1,9,2048]{3,2,0,1:T(8,128)(2,1)S(1)}, bf16[1,1,9,2048]{3,2,0,1:T(8,128)(2,1)S(1)}, u32[]{:S(2)}, u32[]{:S(2)}) collective-permute-start(bf16[1,1,9,2048]{3,2,0,1:T(8,128)(2,1)S(1)} %get-tuple-element.996), channel_id=1, source_target_pairs={{0,6},{2,8},{4,10},{6,12},{8,14},{10,0},{12,2},{14,4},{1,7},{3,9},... | collective-permute-start | bytes 110600 | tf_op jit(solution)/shard_map/while/body/eval_jaxpr/ppermute | solution.py:110
  78.2 8.3 %collective-permute-start.3 = (bf16[1,1,9,2048]{3,2,0,1:T(8,128)(2,1)S(1)}, bf16[1,1,9,2048]{3,2,0,1:T(8,128)(2,1)S(1)}, u32[]{:S(2)}, u32[]{:S(2)}) collective-permute-start(bf16[1,1,9,2048]{3,2,0,1:T(8,128)(2,1)S(1)} %get-tuple-element.997), channel_id=1, source_target_pairs={{0,8},{2,10},{4,12},{6,14},{8,0},{10,2},{12,4},{14,6},{1,9},{3,11}... | collective-permute-start | bytes 110600 | tf_op jit(solution)/shard_map/while/body/eval_jaxpr/ppermute | solution.py:110
  95.9 17.4 %all-to-all-start = ((bf16[8,9,2048]{2,1,0:T(8,128)(2,1)}), bf16[8,9,2048]{2,1,0:T(8,128)(2,1)}, u32[]{:S(2)}, u32[]{:S(2)}) async-start(bf16[8,9,2048]{2,1,0:T(8,128)(2,1)} %reshape.247), calls=%async_computation | async-start | bytes 1048576 | tf_op jit(solution)/shard_map/while/body/eval_jaxpr/all_to_all | solution.py:122
  131.5 9.4 %collective-permute-start.1 = (bf16[1,1,9,2048]{3,2,0,1:T(8,128)(2,1)}, bf16[1,1,9,2048]{3,2,0,1:T(8,128)(2,1)S(1)}, u32[]{:S(2)}, u32[]{:S(2)}) collective-permute-start(bf16[1,1,9,2048]{3,2,0,1:T(8,128)(2,1)} %get-tuple-element.995), channel_id=1, source_target_pairs={{0,4},{2,6},{4,8},{6,10},{8,12},{10,14},{12,0},{14,2},{1,5},{3,7},... | collective-permute-start | bytes 110600 | tf_op jit(solution)/shard_map/while/body/eval_jaxpr/ppermute | solution.py:110
  133.3 8.2 %collective-permute-start.2 = (bf16[1,1,9,2048]{3,2,0,1:T(8,128)(2,1)S(1)}, bf16[1,1,9,2048]{3,2,0,1:T(8,128)(2,1)S(1)}, u32[]{:S(2)}, u32[]{:S(2)}) collective-permute-start(bf16[1,1,9,2048]{3,2,0,1:T(8,128)(2,1)S(1)} %get-tuple-element.996), channel_id=1, source_target_pairs={{0,6},{2,8},{4,10},{6,12},{8,14},{10,0},{12,2},{14,4},{1,7},{3,9},... | collective-permute-start | bytes 110600 | tf_op jit(solution)/shard_map/while/body/eval_jaxpr/ppermute | solution.py:110
  133.3 8.3 %collective-permute-start.3 = (bf16[1,1,9,2048]{3,2,0,1:T(8,128)(2,1)S(1)}, bf16[1,1,9,2048]{3,2,0,1:T(8,128)(2,1)S(1)}, u32[]{:S(2)}, u32[]{:S(2)}) collective-permute-start(bf16[1,1,9,2048]{3,2,0,1:T(8,128)(2,1)S(1)} %get-tuple-element.997), channel_id=1, source_target_pairs={{0,8},{2,10},{4,12},{6,14},{8,0},{10,2},{12,4},{14,6},{1,9},{3,11}... | collective-permute-start | bytes 110600 | tf_op jit(solution)/shard_map/while/body/eval_jaxpr/ppermute | solution.py:110
  151.0 17.4 %all-to-all-start = ((bf16[8,9,2048]{2,1,0:T(8,128)(2,1)}), bf16[8,9,2048]{2,1,0:T(8,128)(2,1)}, u32[]{:S(2)}, u32[]{:S(2)}) async-start(bf16[8,9,2048]{2,1,0:T(8,128)(2,1)} %reshape.247), calls=%async_computation | async-start | bytes 1048576 | tf_op jit(solution)/shard_map/while/body/eval_jaxpr/all_to_all | solution.py:122
  186.6 9.4 %collective-permute-start.1 = (bf16[1,1,9,2048]{3,2,0,1:T(8,128)(2,1)}, bf16[1,1,9,2048]{3,2,0,1:T(8,128)(2,1)S(1)}, u32[]{:S(2)}, u32[]{:S(2)}) collective-permute-start(bf16[1,1,9,2048]{3,2,0,1:T(8,128)(2,1)} %get-tuple-element.995), channel_id=1, source_target_pairs={{0,4},{2,6},{4,8},{6,10},{8,12},{10,14},{12,0},{14,2},{1,5},{3,7},... | collective-permute-start | bytes 110600 | tf_op jit(solution)/shard_map/while/body/eval_jaxpr/ppermute | solution.py:110
  188.3 8.2 %collective-permute-start.2 = (bf16[1,1,9,2048]{3,2,0,1:T(8,128)(2,1)S(1)}, bf16[1,1,9,2048]{3,2,0,1:T(8,128)(2,1)S(1)}, u32[]{:S(2)}, u32[]{:S(2)}) collective-permute-start(bf16[1,1,9,2048]{3,2,0,1:T(8,128)(2,1)S(1)} %get-tuple-element.996), channel_id=1, source_target_pairs={{0,6},{2,8},{4,10},{6,12},{8,14},{10,0},{12,2},{14,4},{1,7},{3,9},... | collective-permute-start | bytes 110600 | tf_op jit(solution)/shard_map/while/body/eval_jaxpr/ppermute | solution.py:110
  188.3 8.3 %collective-permute-start.3 = (bf16[1,1,9,2048]{3,2,0,1:T(8,128)(2,1)S(1)}, bf16[1,1,9,2048]{3,2,0,1:T(8,128)(2,1)S(1)}, u32[]{:S(2)}, u32[]{:S(2)}) collective-permute-start(bf16[1,1,9,2048]{3,2,0,1:T(8,128)(2,1)S(1)} %get-tuple-element.997), channel_id=1, source_target_pairs={{0,8},{2,10},{4,12},{6,14},{8,0},{10,2},{12,4},{14,6},{1,9},{3,11}... | collective-permute-start | bytes 110600 | tf_op jit(solution)/shard_map/while/body/eval_jaxpr/ppermute | solution.py:110
  206.1 17.3 %all-to-all-start = ((bf16[8,9,2048]{2,1,0:T(8,128)(2,1)}), bf16[8,9,2048]{2,1,0:T(8,128)(2,1)}, u32[]{:S(2)}, u32[]{:S(2)}) async-start(bf16[8,9,2048]{2,1,0:T(8,128)(2,1)} %reshape.247), calls=%async_computation | async-start | bytes 1048576 | tf_op jit(solution)/shard_map/while/body/eval_jaxpr/all_to_all | solution.py:122
  241.6 9.4 %collective-permute-start.1 = (bf16[1,1,9,2048]{3,2,0,1:T(8,128)(2,1)}, bf16[1,1,9,2048]{3,2,0,1:T(8,128)(2,1)S(1)}, u32[]{:S(2)}, u32[]{:S(2)}) collective-permute-start(bf16[1,1,9,2048]{3,2,0,1:T(8,128)(2,1)} %get-tuple-element.995), channel_id=1, source_target_pairs={{0,4},{2,6},{4,8},{6,10},{8,12},{10,14},{12,0},{14,2},{1,5},{3,7},... | collective-permute-start | bytes 110600 | tf_op jit(solution)/shard_map/while/body/eval_jaxpr/ppermute | solution.py:110
  243.4 8.2 %collective-permute-start.2 = (bf16[1,1,9,2048]{3,2,0,1:T(8,128)(2,1)S(1)}, bf16[1,1,9,2048]{3,2,0,1:T(8,128)(2,1)S(1)}, u32[]{:S(2)}, u32[]{:S(2)}) collective-permute-start(bf16[1,1,9,2048]{3,2,0,1:T(8,128)(2,1)S(1)} %get-tuple-element.996), channel_id=1, source_target_pairs={{0,6},{2,8},{4,10},{6,12},{8,14},{10,0},{12,2},{14,4},{1,7},{3,9},... | collective-permute-start | bytes 110600 | tf_op jit(solution)/shard_map/while/body/eval_jaxpr/ppermute | solution.py:110
  243.4 8.3 %collective-permute-start.3 = (bf16[1,1,9,2048]{3,2,0,1:T(8,128)(2,1)S(1)}, bf16[1,1,9,2048]{3,2,0,1:T(8,128)(2,1)S(1)}, u32[]{:S(2)}, u32[]{:S(2)}) collective-permute-start(bf16[1,1,9,2048]{3,2,0,1:T(8,128)(2,1)S(1)} %get-tuple-element.997), channel_id=1, source_target_pairs={{0,8},{2,10},{4,12},{6,14},{8,0},{10,2},{12,4},{14,6},{1,9},{3,11}... | collective-permute-start | bytes 110600 | tf_op jit(solution)/shard_map/while/body/eval_jaxpr/ppermute | solution.py:110
  261.1 17.4 %all-to-all-start = ((bf16[8,9,2048]{2,1,0:T(8,128)(2,1)}), bf16[8,9,2048]{2,1,0:T(8,128)(2,1)}, u32[]{:S(2)}, u32[]{:S(2)}) async-start(bf16[8,9,2048]{2,1,0:T(8,128)(2,1)} %reshape.247), calls=%async_computation | async-start | bytes 1048576 | tf_op jit(solution)/shard_map/while/body/eval_jaxpr/all_to_all | solution.py:122
  297.3 17.9 %all-to-all-start.1 = ((bf16[8,9,2048]{2,1,0:T(8,128)(2,1)}), bf16[8,9,2048]{2,1,0:T(8,128)(2,1)S(1)}, u32[]{:S(2)}, u32[]{:S(2)}) async-start(bf16[8,9,2048]{2,1,0:T(8,128)(2,1)} %reshape.250), calls=%async_computation.1 | async-start | bytes 1048576 | tf_op jit(solution)/shard_map/while/body/eval_jaxpr/all_to_all | solution.py:186
  325.1 18.3 %all-to-all-start.2 = ((bf16[8,9,2048]{2,1,0:T(8,128)(2,1)}), bf16[8,9,2048]{2,1,0:T(8,128)(2,1)}, u32[]{:S(2)}, u32[]{:S(2)}) async-start(bf16[8,9,2048]{2,1,0:T(8,128)(2,1)} %reshape.252), calls=%async_computation.2 | async-start | bytes 1048576 | tf_op jit(solution)/shard_map/while/body/eval_jaxpr/all_to_all | solution.py:197
  353.7 19.4 %all-to-all-start.1 = ((bf16[8,9,2048]{2,1,0:T(8,128)(2,1)}), bf16[8,9,2048]{2,1,0:T(8,128)(2,1)S(1)}, u32[]{:S(2)}, u32[]{:S(2)}) async-start(bf16[8,9,2048]{2,1,0:T(8,128)(2,1)} %reshape.250), calls=%async_computation.1 | async-start | bytes 1048576 | tf_op jit(solution)/shard_map/while/body/eval_jaxpr/all_to_all | solution.py:186
  383.0 19.0 %all-to-all-start.2 = ((bf16[8,9,2048]{2,1,0:T(8,128)(2,1)}), bf16[8,9,2048]{2,1,0:T(8,128)(2,1)}, u32[]{:S(2)}, u32[]{:S(2)}) async-start(bf16[8,9,2048]{2,1,0:T(8,128)(2,1)} %reshape.252), calls=%async_computation.2 | async-start | bytes 1048576 | tf_op jit(solution)/shard_map/while/body/eval_jaxpr/all_to_all | solution.py:197
  412.3 19.4 %all-to-all-start.1 = ((bf16[8,9,2048]{2,1,0:T(8,128)(2,1)}), bf16[8,9,2048]{2,1,0:T(8,128)(2,1)S(1)}, u32[]{:S(2)}, u32[]{:S(2)}) async-start(bf16[8,9,2048]{2,1,0:T(8,128)(2,1)} %reshape.250), calls=%async_computation.1 | async-start | bytes 1048576 | tf_op jit(solution)/shard_map/while/body/eval_jaxpr/all_to_all | solution.py:186
  441.6 19.0 %all-to-all-start.2 = ((bf16[8,9,2048]{2,1,0:T(8,128)(2,1)}), bf16[8,9,2048]{2,1,0:T(8,128)(2,1)}, u32[]{:S(2)}, u32[]{:S(2)}) async-start(bf16[8,9,2048]{2,1,0:T(8,128)(2,1)} %reshape.252), calls=%async_computation.2 | async-start | bytes 1048576 | tf_op jit(solution)/shard_map/while/body/eval_jaxpr/all_to_all | solution.py:197
  471.0 19.4 %all-to-all-start.1 = ((bf16[8,9,2048]{2,1,0:T(8,128)(2,1)}), bf16[8,9,2048]{2,1,0:T(8,128)(2,1)S(1)}, u32[]{:S(2)}, u32[]{:S(2)}) async-start(bf16[8,9,2048]{2,1,0:T(8,128)(2,1)} %reshape.250), calls=%async_computation.1 | async-start | bytes 1048576 | tf_op jit(solution)/shard_map/while/body/eval_jaxpr/all_to_all | solution.py:186
  500.3 19.0 %all-to-all-start.2 = ((bf16[8,9,2048]{2,1,0:T(8,128)(2,1)}), bf16[8,9,2048]{2,1,0:T(8,128)(2,1)}, u32[]{:S(2)}, u32[]{:S(2)}) async-start(bf16[8,9,2048]{2,1,0:T(8,128)(2,1)} %reshape.252), calls=%async_computation.2 | async-start | bytes 1048576 | tf_op jit(solution)/shard_map/while/body/eval_jaxpr/all_to_all | solution.py:197
  529.6 19.4 %all-to-all-start.1 = ((bf16[8,9,2048]{2,1,0:T(8,128)(2,1)}), bf16[8,9,2048]{2,1,0:T(8,128)(2,1)S(1)}, u32[]{:S(2)}, u32[]{:S(2)}) async-start(bf16[8,9,2048]{2,1,0:T(8,128)(2,1)} %reshape.250), calls=%async_computation.1 | async-start | bytes 1048576 | tf_op jit(solution)/shard_map/while/body/eval_jaxpr/all_to_all | solution.py:186
  558.9 19.0 %all-to-all-start.2 = ((bf16[8,9,2048]{2,1,0:T(8,128)(2,1)}), bf16[8,9,2048]{2,1,0:T(8,128)(2,1)}, u32[]{:S(2)}, u32[]{:S(2)}) async-start(bf16[8,9,2048]{2,1,0:T(8,128)(2,1)} %reshape.252), calls=%async_computation.2 | async-start | bytes 1048576 | tf_op jit(solution)/shard_map/while/body/eval_jaxpr/all_to_all | solution.py:197
  584.5 40.1 %all-to-all-start.3 = ((bf16[288,2,1024]{2,0,1:T(8,128)(2,1)}), bf16[288,2,1024]{2,0,1:T(8,128)(2,1)}, u32[]{:S(2)}, u32[]{:S(2)}) async-start(bf16[288,2,1024]{2,0,1:T(8,128)(2,1)} %copy.40), calls=%async_computation.3 | async-start | bytes 2359296 | tf_op jit(solution)/shard_map/all_to_all | solution.py:237
  624.7 34.6 %all-to-all-start.4 = ((bf16[288,2,1024]{2,0,1:T(8,128)(2,1)}), bf16[288,2,1024]{2,0,1:T(8,128)(2,1)S(1)}, u32[]{:S(2)}, u32[]{:S(2)}) async-start(bf16[288,2,1024]{2,0,1:T(8,128)(2,1)} %copy.41), calls=%async_computation.4 | async-start | bytes 2359296 | tf_op jit(solution)/shard_map/all_to_all | solution.py:238
  (71 other events, 399.8 us)
